TPU v7x, 32 devices: a whole 2x2x4 slice. The times are simulated.
32 devices in a mesh: groups: 2 (over y), region: 4 (over z), head: 4 (over x, core).
Axes of the slice: x: 2, y: 2, z: 4, core: 2. Of those that a mesh axis runs over, the one named last changes fastest.
Arguments:
- video_queries: bfloat16 [2, 4, 256, 3072], P('groups', 'region', None, 'head'), parts along dimension 0, may hold values from -6 to 6
- video_keys: bfloat16 [2, 4, 256, 3072], P('groups', 'region', None, 'head'), parts along dimension 0, may hold values from -6 to 6
- video_values: bfloat16 [2, 4, 256, 3072], P('groups', 'region', None, 'head'), parts along dimension 0, may hold values from -12 to 12
- head_window: int32 [24, 2], P('head'), may hold values from 0 to 1
- prompt_keys: bfloat16 [512, 3072], P(('groups', 'region'), 'head'), parts along dimension 0, may hold values from -10 to 10
- prompt_values: bfloat16 [512, 3072], P(('groups', 'region'), 'head'), parts along dimension 0, may hold values from -10 to 10
- text_len: int32 [2], P('groups'), parts along dimension 0, may hold values from 64 to 256
Outputs:
- attended: bfloat16 [2, 4, 256, 3072], P('groups', 'region', None, 'head'), parts along dimension 0
There are 2 independent parts, one for each index of `groups`. A program takes and returns all parts, laid end to end along the dimension named above; an argument that names none is the same for every part. Nothing has to cross between parts.
Inputs may be any that keep to these rules, and one draw needn't show every extreme that they name: `head_window`: entry (h, 0) is head h's reach in tiles along grid rows, (h, 1) along grid columns; the window spans 2 r + 1 tiles along each. The first text_len[0] of the 256 prompt tokens are live.
All inputs are finite; a program needn't handle non-finite values.
Results may differ from a plain program's by a relative error of at most 0.0035.
Values may be sent and summed in bfloat16 or wider, within the bound.
A program may use at most 128 MiB of HBM per device.

v0:
```python
import math
import jax
import jax.numpy as jnp
from jax import lax
from jax.sharding import PartitionSpec as P


def absorb(softmax_state, query_heads, block_keys, block_values, allowed):
    running_max, running_sum, weighted = softmax_state
    score_scale = 1.0 / math.sqrt(query_heads.shape[-1])
    scores = (
        jnp.einsum("sqhd,skhd->shqk", query_heads, block_keys, preferred_element_type=jnp.float32)
        * score_scale
    )
    scores = jnp.where(allowed, scores, -jnp.inf)
    new_max = jnp.maximum(running_max, jnp.max(scores, axis=-1, keepdims=True))
    weights = jnp.exp(scores - new_max)
    rescale = jnp.exp(running_max - new_max)
    running_sum = running_sum * rescale + jnp.sum(weights, axis=-1, keepdims=True)
    contribution = jnp.einsum(
        "shqk,skhd->sqhd",
        weights.astype(jnp.bfloat16),
        block_values,
        preferred_element_type=jnp.float32,
    )
    weighted = weighted * jnp.transpose(rescale, (0, 2, 1, 3)) + contribution
    return (new_max, running_sum, weighted)


def shards(
    video_queries, video_keys, video_values, head_window, prompt_keys, prompt_values, text_len
):
    slab_count = video_queries.shape[0]
    tile_tok = video_queries.shape[2]
    features = video_queries.shape[3]
    head_count = head_window.shape[0]
    head_dim = features // head_count
    region_count = lax.axis_size("region")
    grid_cols = min(8, region_count // 2)
    position = lax.axis_index("region")
    my_row = position // grid_cols
    my_col = position % grid_cols
    reach_rows = head_window[:, 0]
    reach_cols = head_window[:, 1]
    query_heads = video_queries.reshape(slab_count, tile_tok, head_count, head_dim)
    paired = jnp.stack([video_keys, video_values])
    stat_shape = (slab_count, head_count, tile_tok, 1)
    softmax_state = (
        jnp.full(stat_shape, -1e30, jnp.float32),
        jnp.zeros(stat_shape, jnp.float32),
        jnp.zeros((slab_count, tile_tok, head_count, head_dim), jnp.float32),
    )
    shard_piece = lax.all_gather(paired, "region", axis=2, tiled=True)
    piece_count = shard_piece.shape[2]

    def one_tile(tile_slot, state_in):
        row_step = tile_slot // grid_cols - my_row
        col_step = tile_slot % grid_cols - my_col
        within = (jnp.abs(row_step) <= reach_rows) & (jnp.abs(col_step) <= reach_cols)
        tile_pair = lax.dynamic_slice_in_dim(shard_piece, tile_slot, 1, 2)
        block_keys = tile_pair[0].reshape(slab_count, tile_tok, head_count, head_dim)
        block_values = tile_pair[1].reshape(slab_count, tile_tok, head_count, head_dim)
        allowed = within.reshape(1, head_count, 1, 1)

        def take_tile(state_keep):
            return absorb(state_keep, query_heads, block_keys, block_values, allowed)

        def keep_state(state_keep):
            return state_keep

        return lax.cond(jnp.any(within), take_tile, keep_state, state_in)

    softmax_state = lax.fori_loop(0, piece_count, one_tile, softmax_state)
    live_text = text_len[0]
    prompt_piece = (
        lax.all_gather(prompt_keys, "region", axis=0, tiled=True),
        lax.all_gather(prompt_values, "region", axis=0, tiled=True),
    )
    piece_count = prompt_piece[0].shape[0]
    block_keys = prompt_piece[0].reshape(1, piece_count, head_count, head_dim)
    block_values = prompt_piece[1].reshape(1, piece_count, head_count, head_dim)
    allowed = (jnp.arange(piece_count, dtype=jnp.int32) < live_text).reshape(1, 1, 1, piece_count)
    softmax_state = absorb(softmax_state, query_heads, block_keys, block_values, allowed)
    running_max, running_sum, weighted = softmax_state
    result = weighted / jnp.transpose(running_sum, (0, 2, 1, 3))
    return result.reshape(slab_count, 1, tile_tok, features).astype(jnp.bfloat16)


def solution(mesh):
    in_specs = (
        P("groups", "region", None, "head"),
        P("groups", "region", None, "head"),
        P("groups", "region", None, "head"),
        P("head", None),
        P(("groups", "region"), "head"),
        P(("groups", "region"), "head"),
        P("groups"),
    )
    out_specs = P("groups", "region", None, "head")
    return jax.shard_map(shards, mesh=mesh, in_specs=in_specs, out_specs=out_specs, check_vma=False)
```

profile of v0, /device:TPU:0, one launch (start us, length us, event | category | flops | bytes accessed | tf_op | source)
XLA Modules:
  0.0 107.9 jit_solution(6140674785394335826)
XLA Ops:
  6.5 0.0 all-gather.2.cloned.1.call-start
  6.5 1.2 %copy.30 = bf16[1,1,256,768]{2,3,1,0:T(8,128)(2,1)S(1)} copy(bf16[1,1,256,768]{3,2,1,0:T(8,128)(2,1)} %param.12) | data formatting | bytes 786432 | tf_op args[1]
  7.7 0.0 copy-start
  7.7 1.2 %copy.31 = bf16[1,1,256,768]{2,3,1,0:T(8,128)(2,1)S(1)} copy(bf16[1,1,256,768]{3,2,1,0:T(8,128)(2,1)} %param.13) | data formatting | bytes 786432 | tf_op args[2]
  8.9 0.9 pad_maximum_fusion
  9.9 0.0 all-gather.2.cloned.1.call-update
  9.9 0.0 copy-start.2
  9.9 0.0 copy-done
  9.9 0.2 copy.32
  10.1 0.0 copy-start.3
  10.1 0.2 copy.33
  10.4 0.4 copy-done.1
  10.8 18.0 %all_gather.10 = bf16[256,768]{1,0:T(8,128)(2,1)S(1)} all-gather(bf16[64,768]{1,0:T(8,128)(2,1)S(1)} %copy-done.1), channel_id=1, replica_groups=mesh['groups'=2,'region'=4,'head'=4] {'region'}, dimensions={0}, use_global_device_ids=true | all-gather | bytes 491520 | tf_op jit(solution)/shard_map/all_gather | solution.py:76
  28.8 0.2 copy.35
  29.6 0.0 copy-done.2
  29.6 20.2 %all_gather.11 = bf16[256,768]{1,0:T(8,128)(2,1)S(1)} all-gather(bf16[64,768]{1,0:T(8,128)(2,1)S(1)} %copy-done.2), channel_id=1, replica_groups=mesh['groups'=2,'region'=4,'head'=4] {'region'}, dimensions={0}, use_global_device_ids=true | all-gather | bytes 491520 | tf_op jit(solution)/shard_map/all_gather | solution.py:77
  49.8 0.2 copy.38
  50.0 0.4 fusion.18
  50.5 33.3 %all-gather.2.cloned.1.call-done = bf16[2,1,4,256,768]{3,4,2,1,0:T(8,128)(2,1)} async-done(((bf16[2,1,1,256,768]{3,4,2,1,0:T(8,128)(2,1)}), bf16[2,1,4,256,768]{3,4,2,1,0:T(8,128)(2,1)}) %all-gather.2.cloned.1.call-update) | async-done | bytes 3145744 | tf_op jit(solution)/shard_map/all_gather | solution.py:53
  83.8 0.1 broadcast_in_dim.51
  83.9 15.6 %while.19 = (s32[]{:T(128)}, f32[1,6,256,1]{2,1,3,0:T(8,128)S(1)}, f32[1,6,256,1]{2,1,3,0:T(8,128)S(1)}, f32[1,256,6,128]{1,3,2,0:T(8,128)S(1)}, s32[]{:T(128)},...) while((s32[]{:T(128)}, f32[1,6,256,1]{2,1,3,0:T(8,128)S(1)}, ...), condition=%wide.region_6.7_spmd, body=%wide.region_0.6_spmd.sunk | while | flops 204476992 | bytes 9142846 | solution.py:73
  83.9 0.7 and_reduce_fusion.2
  85.3 2.5 %conditional.2 = ((f32[1,6,256,1]{2,1,3,0:T(8,128)S(1)}, f32[1,6,256,1]{2,1,3,0:T(8,128)S(1)}, f32[1,256,6,128]{1,3,2,0:T(8,128)S(1)})) conditional(s32[]{:T(128)} %convert_element_type.43, (f32[1,6,256,1]{2,1,3,0:T(8,128)S(1)}, f32[1,6,256,1]{2,1,3,0:T(8,128)S(1)}, f32[1,256,6,128]{1,3,2,0:T(8,128)S(1)}) %tuple.58, (s32[]{:T(128)}, s32[6]{0:T(128)S(1)}, ...), branch_computations={%region_2.2_spmd, %region_3.5_spmd} | conditional | flops 204476944 | bytes 9142392 | solution.py:71
  85.3 1.2 %constant_dynamic-slice_fusion.1 = (bf16[1,1,1,256,768]{3,4,2,1,0:T(8,128)(2,1)S(1)}, bf16[1,1,1,256,768]{3,4,2,1,0:T(8,128)(2,1)S(1)}) fusion(bf16[2,1,4,256,768]{3,4,2,1,0:T(8,128)(2,1)} %get-tuple-element.353, s32[]{:T(128)S(6)} %add.74, s32[]{:T(128)} %get-tuple-element.354), kind=kLoop, calls=%fused_computation.16 | loop fusion | bytes 1572872 | tf_op jit(solution)/shard_map/while/body/eval_jaxpr/slice | solution.py:62
  86.5 0.4 bitcast_reduce_fusion
  86.9 0.2 fusion.2
  87.2 0.6 fusion.3
  87.8 0.7 and_reduce_fusion.2
  89.2 2.5 %conditional.2 = ((f32[1,6,256,1]{2,1,3,0:T(8,128)S(1)}, f32[1,6,256,1]{2,1,3,0:T(8,128)S(1)}, f32[1,256,6,128]{1,3,2,0:T(8,128)S(1)})) conditional(s32[]{:T(128)} %convert_element_type.43, (f32[1,6,256,1]{2,1,3,0:T(8,128)S(1)}, f32[1,6,256,1]{2,1,3,0:T(8,128)S(1)}, f32[1,256,6,128]{1,3,2,0:T(8,128)S(1)}) %tuple.58, (s32[]{:T(128)}, s32[6]{0:T(128)S(1)}, ...), branch_computations={%region_2.2_spmd, %region_3.5_spmd} | conditional | flops 204476944 | bytes 9142392 | solution.py:71
  89.2 1.2 %constant_dynamic-slice_fusion.1 = (bf16[1,1,1,256,768]{3,4,2,1,0:T(8,128)(2,1)S(1)}, bf16[1,1,1,256,768]{3,4,2,1,0:T(8,128)(2,1)S(1)}) fusion(bf16[2,1,4,256,768]{3,4,2,1,0:T(8,128)(2,1)} %get-tuple-element.353, s32[]{:T(128)S(6)} %add.74, s32[]{:T(128)} %get-tuple-element.354), kind=kLoop, calls=%fused_computation.16 | loop fusion | bytes 1572872 | tf_op jit(solution)/shard_map/while/body/eval_jaxpr/slice | solution.py:62
  90.4 0.4 bitcast_reduce_fusion
  90.8 0.2 fusion.2
  91.1 0.6 fusion.3
  91.7 0.7 and_reduce_fusion.2
  93.1 2.5 %conditional.2 = ((f32[1,6,256,1]{2,1,3,0:T(8,128)S(1)}, f32[1,6,256,1]{2,1,3,0:T(8,128)S(1)}, f32[1,256,6,128]{1,3,2,0:T(8,128)S(1)})) conditional(s32[]{:T(128)} %convert_element_type.43, (f32[1,6,256,1]{2,1,3,0:T(8,128)S(1)}, f32[1,6,256,1]{2,1,3,0:T(8,128)S(1)}, f32[1,256,6,128]{1,3,2,0:T(8,128)S(1)}) %tuple.58, (s32[]{:T(128)}, s32[6]{0:T(128)S(1)}, ...), branch_computations={%region_2.2_spmd, %region_3.5_spmd} | conditional | flops 204476944 | bytes 9142392 | solution.py:71
  93.1 1.2 %constant_dynamic-slice_fusion.1 = (bf16[1,1,1,256,768]{3,4,2,1,0:T(8,128)(2,1)S(1)}, bf16[1,1,1,256,768]{3,4,2,1,0:T(8,128)(2,1)S(1)}) fusion(bf16[2,1,4,256,768]{3,4,2,1,0:T(8,128)(2,1)} %get-tuple-element.353, s32[]{:T(128)S(6)} %add.74, s32[]{:T(128)} %get-tuple-element.354), kind=kLoop, calls=%fused_computation.16 | loop fusion | bytes 1572872 | tf_op jit(solution)/shard_map/while/body/eval_jaxpr/slice | solution.py:62
  94.3 0.4 bitcast_reduce_fusion
  94.7 0.2 fusion.2
  95.0 0.6 fusion.3
  95.6 0.7 and_reduce_fusion.2
  97.0 2.5 %conditional.2 = ((f32[1,6,256,1]{2,1,3,0:T(8,128)S(1)}, f32[1,6,256,1]{2,1,3,0:T(8,128)S(1)}, f32[1,256,6,128]{1,3,2,0:T(8,128)S(1)})) conditional(s32[]{:T(128)} %convert_element_type.43, (f32[1,6,256,1]{2,1,3,0:T(8,128)S(1)}, f32[1,6,256,1]{2,1,3,0:T(8,128)S(1)}, f32[1,256,6,128]{1,3,2,0:T(8,128)S(1)}) %tuple.58, (s32[]{:T(128)}, s32[6]{0:T(128)S(1)}, ...), branch_computations={%region_2.2_spmd, %region_3.5_spmd} | conditional | flops 204476944 | bytes 9142392 | solution.py:71
  97.0 1.2 %constant_dynamic-slice_fusion.1 = (bf16[1,1,1,256,768]{3,4,2,1,0:T(8,128)(2,1)S(1)}, bf16[1,1,1,256,768]{3,4,2,1,0:T(8,128)(2,1)S(1)}) fusion(bf16[2,1,4,256,768]{3,4,2,1,0:T(8,128)(2,1)} %get-tuple-element.353, s32[]{:T(128)S(6)} %add.74, s32[]{:T(128)} %get-tuple-element.354), kind=kLoop, calls=%fused_computation.16 | loop fusion | bytes 1572872 | tf_op jit(solution)/shard_map/while/body/eval_jaxpr/slice | solution.py:62
  98.2 0.4 bitcast_reduce_fusion
  98.6 0.2 fusion.2
  98.9 0.6 fusion.3
  99.5 0.2 fusion.8
  99.7 0.4 fusion.12
  100.2 0.9 copy.40
  (24 shorter events, 0.2 us)
Async XLA Ops:
  6.5 77.2 %all-gather.2.cloned.1.call-start = ((), (), s32[]{:S(2)}) async-start(), calls=%async_computation | async-start | bytes 3932160 | tf_op jit(solution)/shard_map/all_gather | solution.py:53
  7.7 2.2 %copy-start = (bf16[1,1,256,768]{3,2,1,0:T(8,128)(2,1)S(1)}, bf16[1,1,256,768]{3,2,1,0:T(8,128)(2,1)}, u32[]{:S(2)}) copy-start(bf16[1,1,256,768]{3,2,1,0:T(8,128)(2,1)} %param.11) | copy-start | bytes 1179652
  9.9 0.9 copy-start.1
  9.9 19.7 %copy-start.2 = (bf16[64,768]{1,0:T(8,128)(2,1)S(1)}, bf16[64,768]{1,0:T(8,128)(2,1)}, u32[]{:S(2)}) copy-start(bf16[64,768]{1,0:T(8,128)(2,1)} %param.16) | copy-start | bytes 294916
  10.1 39.9 %copy-start.3 = (s32[6,2]{0,1:T(2,128)S(1)}, s32[6,2]{0,1:T(2,128)}, u32[]{:S(2)}) copy-start(s32[6,2]{0,1:T(2,128)} %param.14) | copy-start | bytes 148
Sparse Core Ops, SparseCore 0:
  10.0 73.7 all-gather.1
where the time goes:
time: 108 us
  blocking collectives  38.2 us (35%)
  waiting for transfers between devices  33.3 us (31%)
  between operations  14.2 us (13%)
  local copies, waits for them, and re-layouts  9.24 us (9%)
  other arithmetic  4.98 us (5%)
  matrix products  4.77 us (4%)
  loops' own time  3.17 us (3%)
    all_gather x1, waiting for transfers between devices, shards(): shard_piece = lax.all_gather(paired, 'region', axis=2, tiled=True)  33.3 us
    all_gather x1, blocking collectives, shards(): lax.all_gather(prompt_values, 'region', axis=0, tiled=True)  20.2 us
    all_gather x1, blocking collectives, shards(): lax.all_gather(prompt_keys, 'region', axis=0, tiled=True)  18 us
    slice x4, local copies, waits for them, and re-layouts, one_tile(): tile_pair[1].reshape(slab_count, tile_tok, head_count, head_dim)  4.7 us
    unnamed x11, local copies, waits for them, and re-layouts  2.98 us
    another operation x1, loops' own time, shards(): softmax_state = lax.fori_loop(0, piece_count, one_tile, softmax_state)  2.89 us
    reduce_or x4, other arithmetic, one_tile(): return lax.cond(jnp.any(within), take_tile, keep_state, state_in)  2.79 us
    dot_general x5, matrix products, absorb(): jnp.einsum('shqk,skhd->sqhd', weights.astype(jnp.bfloat16), block_values,...  2.63 us
  transfers between devices with their start and end apart: 1, of which 1 were waited for; matrix products, arithmetic and copies ran while one was open for 1% of the time, Pallas kernels for 0%

commit v1 on v0

--- a/solution.py
+++ b/solution.py
@@ -50,7 +50,14 @@
         jnp.zeros(stat_shape, jnp.float32),
         jnp.zeros((slab_count, tile_tok, head_count, head_dim), jnp.float32),
     )
-    shard_piece = lax.all_gather(paired, "region", axis=2, tiled=True)
+    ring = [paired]
+    for hop in range(3):
+        ring.append(lax.ppermute(ring[-1], "region", [(dev, (dev + 1) % 4) for dev in range(4)]))
+    shard_piece = jnp.roll(
+        jnp.concatenate(ring[::-1], axis=2),
+        (lax.axis_index("region") + 1) * ring[0].shape[2],
+        axis=2,
+    )
     piece_count = shard_piece.shape[2]
 
     def one_tile(tile_slot, state_in):

time: 108 us -> 120 us (1.11)
  between operations: 14.2 us -> 0.87 us
  local copies, waits for them, and re-layouts: 9.24 us -> 18 us
  waiting for transfers between devices: 33.3 us -> 40.2 us
  blocking collectives: 38.2 us -> 45.1 us
  starting transfers between devices: 0.01 us -> 3.11 us
    ppermute x0 -> x3, waiting for transfers between devices: none -> 40.2 us  [shards(): lax.ppermute(ring[-1], 'region', [(dev, (dev + 1) % 4) for dev in range(4)])]
    all_gather x1 -> x0, waiting for transfers between devices: 33.3 us -> none  [shards(): shard_piece = lax.all_gather(paired, 'region', axis=2, tiled=True)]
    all_gather x1, blocking collectives: 18 us -> 30.6 us  [shards(): lax.all_gather(prompt_keys, 'region', axis=0, tiled=True)]
    unnamed x11 -> x23, local copies, waits for them, and re-layouts: 2.98 us -> 9.15 us
    all_gather x1, blocking collectives: 20.2 us -> 14.5 us  [shards(): lax.all_gather(prompt_values, 'region', axis=0, tiled=True)]
    ppermute x0 -> x3, starting transfers between devices: none -> 3.11 us  [shards(): lax.ppermute(ring[-1], 'region', [(dev, (dev + 1) % 4) for dev in range(4)])]
    dynamic_slice x0 -> x1, local copies, waits for them, and re-layouts: none -> 1.87 us  [shards(): jnp.roll(jnp.concatenate(ring[::-1], axis=2), (lax.axis_index('region') +...]
  transfers between devices with their start and end apart: 1 -> 3, of which waited for: 1 -> 2; matrix products, arithmetic and copies ran while one was open for 1% -> 2% of each run, Pallas kernels for 0% -> 0%
where the time goes in v1:
time: 120 us; the launch traced here: 119 us
  blocking collectives  45.1 us (38%)
  waiting for transfers between devices  40.2 us (34%)
  local copies, waits for them, and re-layouts  18 us (15%)
  matrix products  4.78 us (4%)
  other arithmetic  4.22 us (4%)
  starting transfers between devices  3.11 us (3%)
  loops' own time  3.01 us (3%)
    ppermute x3, waiting for transfers between devices, shards(): lax.ppermute(ring[-1], 'region', [(dev, (dev + 1) % 4) for dev in range(4)])  40.2 us
    all_gather x1, blocking collectives, shards(): lax.all_gather(prompt_keys, 'region', axis=0, tiled=True)  30.6 us
    all_gather x1, blocking collectives, shards(): lax.all_gather(prompt_values, 'region', axis=0, tiled=True)  14.5 us
    unnamed x23, local copies, waits for them, and re-layouts  9.15 us
    slice x4, local copies, waits for them, and re-layouts, one_tile(): tile_pair[1].reshape(slab_count, tile_tok, head_count, head_dim)  4.7 us
    ppermute x3, starting transfers between devices, shards(): lax.ppermute(ring[-1], 'region', [(dev, (dev + 1) % 4) for dev in range(4)])  3.11 us
    reduce_or x4, other arithmetic, one_tile(): return lax.cond(jnp.any(within), take_tile, keep_state, state_in)  2.8 us
    another operation x1, loops' own time, shards(): softmax_state = lax.fori_loop(0, piece_count, one_tile, softmax_state)  2.73 us
  transfers between devices with their start and end apart: 3, of which 2 were waited for; matrix products, arithmetic and copies ran while one was open for 2% of the time, Pallas kernels for 0%

profile of v1, /device:TPU:0, one launch (start us, length us, event | category | flops | bytes accessed | tf_op | source)
XLA Modules:
  0.0 119.3 jit_solution(6075496878303848204)
XLA Ops:
  0.0 1.2 %copy.30 = bf16[1,1,256,768]{2,3,1,0:T(8,128)(2,1)S(1)} copy(bf16[1,1,256,768]{3,2,1,0:T(8,128)(2,1)} %param.12) | data formatting | bytes 786432 | tf_op args[1]
  1.2 1.2 %copy.31 = bf16[1,1,256,768]{2,3,1,0:T(8,128)(2,1)S(1)} copy(bf16[1,1,256,768]{3,2,1,0:T(8,128)(2,1)} %param.13) | data formatting | bytes 786432 | tf_op args[2]
  2.4 0.1 pad_maximum_fusion
  2.5 3.1 %collective-permute-start = (bf16[2,1,1,256,768]{3,4,2,1,0:T(8,128)(2,1)S(1)}, bf16[2,1,1,256,768]{3,4,2,1,0:T(8,128)(2,1)S(1)}, u32[]{:S(2)}, u32[]{:S(2)}) collective-permute-start(bf16[2,1,1,256,768]{3,4,2,1,0:T(8,128)(2,1)S(1)} %pad_maximum_fusion), channel_id=1, source_target_pairs={{0,4},{4,8},{8,12},{12,0},{1,5},{5,9},{9,13},{13,1},{2,6},{6,10},{... | collective-permute-start | bytes 2359304 | tf_op jit(solution)/shard_map/ppermute | solution.py:55
  5.6 19.6 %collective-permute-done = bf16[2,1,1,256,768]{3,4,2,1,0:T(8,128)(2,1)S(1)} collective-permute-done((bf16[2,1,1,256,768]{3,4,2,1,0:T(8,128)(2,1)S(1)}, bf16[2,1,1,256,768]{3,4,2,1,0:T(8,128)(2,1)S(1)}, u32[]{:S(2)}, u32[]{:S(2)}) %collective-permute-start) | collective-permute-done | bytes 786464 | tf_op jit(solution)/shard_map/ppermute | solution.py:55
  25.2 0.9 copy-done
  26.1 20.6 %collective-permute-done.1 = bf16[2,1,1,256,768]{3,4,2,1,0:T(8,128)(2,1)} collective-permute-done((bf16[2,1,1,256,768]{3,4,2,1,0:T(8,128)(2,1)S(1)}, bf16[2,1,1,256,768]{3,4,2,1,0:T(8,128)(2,1)}, u32[]{:S(2)}, u32[]{:S(2)}) %collective-permute-start.1) | collective-permute-done | bytes 786464 | tf_op jit(solution)/shard_map/ppermute | solution.py:55
  46.7 30.6 %all_gather.6 = bf16[256,768]{1,0:T(8,128)(2,1)S(1)} all-gather(bf16[64,768]{1,0:T(8,128)(2,1)S(1)} %copy-done.4), channel_id=1, replica_groups=mesh['groups'=2,'region'=4,'head'=4] {'region'}, dimensions={0}, use_global_device_ids=true | all-gather | bytes 491520 | tf_op jit(solution)/shard_map/all_gather | solution.py:83
  77.3 0.2 copy.32
  77.5 0.2 copy.33
  77.7 0.2 copy.35
  78.5 14.5 %all_gather.7 = bf16[256,768]{1,0:T(8,128)(2,1)S(1)} all-gather(bf16[64,768]{1,0:T(8,128)(2,1)S(1)} %copy-done.5), channel_id=1, replica_groups=mesh['groups'=2,'region'=4,'head'=4] {'region'}, dimensions={0}, use_global_device_ids=true | all-gather | bytes 491520 | tf_op jit(solution)/shard_map/all_gather | solution.py:84
  93.1 0.9 copy.38
  94.0 0.4 fusion.18
  94.5 1.3 %constant_dynamic-update-slice_fusion.7 = bf16[2,1,8,256,768]{3,4,2,1,0:T(8,128)(2,1)S(1)} fusion(bf16[2,1,1,256,768]{3,4,2,1,0:T(8,128)(2,1)} %collective-permute-done.2), kind=kLoop, calls=%fused_computation.35 | loop fusion | bytes 1572864
  95.7 1.2 constant_dynamic-update-slice_fusion.6
  97.0 1.2 constant_dynamic-update-slice_fusion.3
  98.2 1.2 constant_dynamic-update-slice_fusion.2
  99.5 1.9 %constant_dynamic-slice_fusion.2 = bf16[2,1,4,256,768]{3,4,2,1,0:T(8,128)(2,1)} fusion(bf16[2,1,8,256,768]{3,4,2,1,0:T(8,128)(2,1)S(1)} %constant_dynamic-update-slice_fusion, s32[]{:T(128)S(6)} %select_n.86), kind=kLoop, calls=%fused_computation.45 | loop fusion | bytes 6291460 | tf_op jit(solution)/shard_map/jit(_roll_dynamic)/dynamic_slice | solution.py:56
  101.5 15.5 %while.19 = (s32[]{:T(128)}, f32[1,6,256,1]{2,1,3,0:T(8,128)S(1)}, f32[1,6,256,1]{2,1,3,0:T(8,128)S(1)}, f32[1,256,6,128]{1,3,2,0:T(8,128)S(1)}, s32[]{:T(128)},...) while((s32[]{:T(128)}, f32[1,6,256,1]{2,1,3,0:T(8,128)S(1)}, ...), condition=%wide.region_6.7_spmd, body=%wide.region_0.6_spmd.sunk | while | flops 204476992 | bytes 9142846 | solution.py:80
  101.5 0.7 and_reduce_fusion.2
  102.9 2.5 %conditional.2 = ((f32[1,6,256,1]{2,1,3,0:T(8,128)S(1)}, f32[1,6,256,1]{2,1,3,0:T(8,128)S(1)}, f32[1,256,6,128]{1,3,2,0:T(8,128)S(1)})) conditional(s32[]{:T(128)} %convert_element_type.43, (f32[1,6,256,1]{2,1,3,0:T(8,128)S(1)}, f32[1,6,256,1]{2,1,3,0:T(8,128)S(1)}, f32[1,256,6,128]{1,3,2,0:T(8,128)S(1)}) %tuple.58, (s32[]{:T(128)}, s32[6]{0:T(128)S(1)}, ...), branch_computations={%region_2.2_spmd, %region_3.5_spmd} | conditional | flops 204476944 | bytes 9142392 | solution.py:78
  102.9 1.2 constant_dynamic-slice_fusion.1
  104.1 0.4 bitcast_reduce_fusion
  104.5 0.2 fusion.2
  104.8 0.6 fusion.3
  105.4 0.7 and_reduce_fusion.2
  106.7 2.5 %conditional.2 = ((f32[1,6,256,1]{2,1,3,0:T(8,128)S(1)}, f32[1,6,256,1]{2,1,3,0:T(8,128)S(1)}, f32[1,256,6,128]{1,3,2,0:T(8,128)S(1)})) conditional(s32[]{:T(128)} %convert_element_type.43, (f32[1,6,256,1]{2,1,3,0:T(8,128)S(1)}, f32[1,6,256,1]{2,1,3,0:T(8,128)S(1)}, f32[1,256,6,128]{1,3,2,0:T(8,128)S(1)}) %tuple.58, (s32[]{:T(128)}, s32[6]{0:T(128)S(1)}, ...), branch_computations={%region_2.2_spmd, %region_3.5_spmd} | conditional | flops 204476944 | bytes 9142392 | solution.py:78
  106.7 1.2 constant_dynamic-slice_fusion.1
  107.9 0.4 bitcast_reduce_fusion
  108.4 0.2 fusion.2
  108.6 0.6 fusion.3
  109.3 0.7 and_reduce_fusion.2
  110.6 2.5 %conditional.2 = ((f32[1,6,256,1]{2,1,3,0:T(8,128)S(1)}, f32[1,6,256,1]{2,1,3,0:T(8,128)S(1)}, f32[1,256,6,128]{1,3,2,0:T(8,128)S(1)})) conditional(s32[]{:T(128)} %convert_element_type.43, (f32[1,6,256,1]{2,1,3,0:T(8,128)S(1)}, f32[1,6,256,1]{2,1,3,0:T(8,128)S(1)}, f32[1,256,6,128]{1,3,2,0:T(8,128)S(1)}) %tuple.58, (s32[]{:T(128)}, s32[6]{0:T(128)S(1)}, ...), branch_computations={%region_2.2_spmd, %region_3.5_spmd} | conditional | flops 204476944 | bytes 9142392 | solution.py:78
  110.6 1.2 constant_dynamic-slice_fusion.1
  111.8 0.4 bitcast_reduce_fusion
  112.3 0.2 fusion.2
  112.5 0.6 fusion.3
  113.1 0.7 and_reduce_fusion.2
  114.5 2.5 %conditional.2 = ((f32[1,6,256,1]{2,1,3,0:T(8,128)S(1)}, f32[1,6,256,1]{2,1,3,0:T(8,128)S(1)}, f32[1,256,6,128]{1,3,2,0:T(8,128)S(1)})) conditional(s32[]{:T(128)} %convert_element_type.43, (f32[1,6,256,1]{2,1,3,0:T(8,128)S(1)}, f32[1,6,256,1]{2,1,3,0:T(8,128)S(1)}, f32[1,256,6,128]{1,3,2,0:T(8,128)S(1)}) %tuple.58, (s32[]{:T(128)}, s32[6]{0:T(128)S(1)}, ...), branch_computations={%region_2.2_spmd, %region_3.5_spmd} | conditional | flops 204476944 | bytes 9142392 | solution.py:78
  114.5 1.2 constant_dynamic-slice_fusion.1
  115.7 0.4 bitcast_reduce_fusion
  116.1 0.2 fusion.2
  116.4 0.6 fusion.3
  117.0 0.2 fusion.8
  117.2 0.7 copy-done.3
  118.0 0.4 fusion.12
  118.4 0.9 copy.40
  (42 shorter events, 0.5 us)
Async XLA Ops:
  0.0 46.7 %copy-start.4 = (bf16[64,768]{1,0:T(8,128)(2,1)S(1)}, bf16[64,768]{1,0:T(8,128)(2,1)}, u32[]{:S(2)}) copy-start(bf16[64,768]{1,0:T(8,128)(2,1)} %param.15) | copy-start | bytes 294916
  1.2 76.1 %copy-start.2 = (bf16[1,1,256,768]{3,2,1,0:T(8,128)(2,1)S(1)}, bf16[1,1,256,768]{3,2,1,0:T(8,128)(2,1)}, u32[]{:S(2)}) copy-start(bf16[1,1,256,768]{3,2,1,0:T(8,128)(2,1)} %param.11) | copy-start | bytes 1179652
  2.5 76.0 %copy-start.5 = (bf16[64,768]{1,0:T(8,128)(2,1)S(1)}, bf16[64,768]{1,0:T(8,128)(2,1)}, u32[]{:S(2)}) copy-start(bf16[64,768]{1,0:T(8,128)(2,1)} %param.16) | copy-start | bytes 294916
  2.5 22.7 %collective-permute-start = (bf16[2,1,1,256,768]{3,4,2,1,0:T(8,128)(2,1)S(1)}, bf16[2,1,1,256,768]{3,4,2,1,0:T(8,128)(2,1)S(1)}, u32[]{:S(2)}, u32[]{:S(2)}) collective-permute-start(bf16[2,1,1,256,768]{3,4,2,1,0:T(8,128)(2,1)S(1)} %pad_maximum_fusion), channel_id=1, source_target_pairs={{0,4},{4,8},{8,12},{12,0},{1,5},{5,9},{9,13},{13,1},{2,6},{6,10},{... | collective-permute-start | bytes 2359304 | tf_op jit(solution)/shard_map/ppermute | solution.py:55
  25.2 0.9 copy-start
  26.1 20.6 %collective-permute-start.1 = (bf16[2,1,1,256,768]{3,4,2,1,0:T(8,128)(2,1)S(1)}, bf16[2,1,1,256,768]{3,4,2,1,0:T(8,128)(2,1)}, u32[]{:S(2)}, u32[]{:S(2)}) collective-permute-start(bf16[2,1,1,256,768]{3,4,2,1,0:T(8,128)(2,1)S(1)} %collective-permute-done), channel_id=1, source_target_pairs={{0,4},{4,8},{8,12},{12,0},{1,5},{5,9},{9,13},{13,1},{2,6},{6,10},{... | collective-permute-start | bytes 2359304 | tf_op jit(solution)/shard_map/ppermute | solution.py:55
  46.7 47.7 %collective-permute-start.2 = (bf16[2,1,1,256,768]{3,4,2,1,0:T(8,128)(2,1)}, bf16[2,1,1,256,768]{3,4,2,1,0:T(8,128)(2,1)}, u32[]{:S(2)}, u32[]{:S(2)}) collective-permute-start(bf16[2,1,1,256,768]{3,4,2,1,0:T(8,128)(2,1)} %collective-permute-done.1), channel_id=1, source_target_pairs={{0,4},{4,8},{8,12},{12,0},{1,5},{5,9},{9,13},{13,1},{2,6},{6,10},{... | collective-permute-start | bytes 2359304 | tf_op jit(solution)/shard_map/ppermute | solution.py:55
  77.5 16.5 %copy-start.6 = (s32[6,2]{0,1:T(2,128)S(1)}, s32[6,2]{0,1:T(2,128)}, u32[]{:S(2)}) copy-start(s32[6,2]{0,1:T(2,128)} %param.14) | copy-start | bytes 148
  94.4 2.5 %copy-start.1 = (bf16[2,1,1,256,768]{3,4,2,1,0:T(8,128)(2,1)S(1)}, bf16[2,1,1,256,768]{3,4,2,1,0:T(8,128)(2,1)}, u32[]{:S(2)}) copy-start(bf16[2,1,1,256,768]{3,4,2,1,0:T(8,128)(2,1)} %copy-done) | copy-start | bytes 2359300
  117.0 1.0 copy-start.3
